TPU v7x, 32 devices: a whole 2x2x4 slice. The times are simulated.
32 devices in a mesh: groups: 2 (over x), fsdp: 8 (over z, y), dp: 2 (over core).
Axes of the slice: x: 2, y: 2, z: 4, core: 2. Of those that a mesh axis runs over, the one named last changes fastest.
Arguments:
- resid: bfloat16 [512, 5120], P(('groups', 'dp'), 'fsdp'), parts along dimension 0, may hold values from -6 to 6
- hidden_act: bfloat16 [512, 6912], P(('groups', 'dp')), parts along dimension 0, may hold values from -11 to 11
- w_down: bfloat16 [6912, 5120], P(None, 'fsdp'), may hold values from -0.078125 to 0.078125
- norm_gain: bfloat16 [5120], P('fsdp'), may hold values from 0.3 to 4, as said below
- head: bfloat16 [5120, 16384], P(None, 'fsdp'), may hold values from -0.25 to 0.25
- data_ids: int32 [512], P(('groups', 'dp')), parts along dimension 0, may hold values from 0 to 16383
- pseudo_ids: int32 [512], P(('groups', 'dp')), parts along dimension 0, may hold values from 0 to 16383
Outputs:
- scores: float32 [512], P(('groups', 'dp')), parts along dimension 0
There are 2 independent parts, one for each index of `groups`. A program takes and returns all parts, laid end to end along the dimension named above; an argument that names none is the same for every part. Nothing has to cross between parts.
Inputs may be any that keep to these rules, and one draw needn't show every extreme that they name: `norm_gain`: positive gains.
All inputs are finite; a program needn't handle non-finite values.
Results may differ from a plain program's by a relative error of at most 0.012.
Values may be sent and summed in bfloat16 or wider, within the bound.
No kernel may reach another device: no remote copies, remote signals or barrier semaphores. Data moves between devices by JAX's collectives and lax.ppermute only.
A program may use at most 192 MiB of HBM per device.

v0:
```python
import jax
import jax.numpy as jnp
from jax import lax
from jax.sharding import PartitionSpec as P

ITERS = 3
cap_value = 30.0
norm_eps = 1e-05
damping = 0.05


def row_total(values):
    return lax.psum(values, "fsdp")


def per_device(resid, hidden_act, w_down, norm_gain, head, data_ids, pseudo_ids):
    tok_rows = hidden_act.shape[0]
    total_rows = tok_rows * lax.axis_size("dp")
    shard_cols = w_down.shape[1]
    width = shard_cols * lax.axis_size("fsdp")
    vocab_cols = head.shape[1]
    vocab_ids = lax.axis_index("fsdp") * vocab_cols + lax.broadcasted_iota(
        jnp.int32, (1, vocab_cols), 1
    )
    gain = norm_gain.astype(jnp.float32)

    def head_logits(normed_shard):
        return jnp.dot(
            lax.all_gather(normed_shard, "fsdp", axis=1, tiled=True),
            head,
            preferred_element_type=jnp.float32,
        )

    def head_project(weighted):
        return (
            lax.psum_scatter(
                lax.dot_general(
                    head, weighted, (((1,), (1,)), ((), ())), preferred_element_type=jnp.float32
                ).astype(jnp.bfloat16),
                "fsdp",
                scatter_dimension=0,
                tiled=True,
            )
            .astype(jnp.float32)
            .T
        )

    z = resid.astype(jnp.float32) + jnp.dot(hidden_act, w_down, preferred_element_type=jnp.float32)
    inv = lax.rsqrt(row_total(jnp.sum(z * z, axis=1, keepdims=True)) / width + norm_eps)
    normed = (z * inv * gain).astype(jnp.bfloat16)
    capped = cap_value * jnp.tanh(head_logits(normed) / cap_value)
    slope = 1.0 - (capped / cap_value) ** 2
    expval = jnp.exp(capped)
    prob = expval / row_total(jnp.sum(expval, axis=1, keepdims=True))

    def norm_back(upstream):
        scaled = gain * head_project((upstream * slope).astype(jnp.bfloat16))
        mixed = row_total(jnp.sum(z * scaled, axis=1, keepdims=True)) / width
        return inv * scaled - z * inv**3 * mixed

    def tangent(full_vector):
        zv = jnp.dot(hidden_act, full_vector, preferred_element_type=jnp.float32)
        inv_t = -(inv**3) * row_total(jnp.sum(z * zv, axis=1, keepdims=True)) / width
        moved = (gain * (zv * inv + z * inv_t)).astype(jnp.bfloat16)
        return slope * head_logits(moved)

    def full_rows(vector):
        return lax.all_gather(vector.astype(jnp.bfloat16), "dp", axis=0, tiled=True)

    def param_sum(dz):
        local = lax.dot_general(
            hidden_act,
            dz.astype(jnp.bfloat16),
            (((0,), (0,)), ((), ())),
            preferred_element_type=jnp.float32,
        )
        return lax.psum_scatter(
            local.astype(jnp.bfloat16), "dp", scatter_dimension=0, tiled=True
        ).astype(jnp.float32)

    def global_dot(values):
        return lax.psum(values, ("fsdp", "dp"))

    pseudo_hot = (pseudo_ids[:, None] == vocab_ids).astype(jnp.float32)
    grad = param_sum(norm_back((prob - pseudo_hot) / total_rows))
    solution = jnp.zeros_like(grad)
    remain = grad
    search = grad
    norm_now = global_dot(jnp.sum(remain * remain))
    for step in range(ITERS):
        change = tangent(full_rows(search))
        inner = row_total(jnp.sum(prob * change, axis=1, keepdims=True))
        image = param_sum(norm_back((prob * change - prob * inner) / total_rows)) + damping * search
        alpha = norm_now / global_dot(jnp.sum(search * image))
        solution = solution + alpha * search
        remain = remain - alpha * image
        if step + 1 < ITERS:
            norm_next = global_dot(jnp.sum(remain * remain))
            search = remain + norm_next / norm_now * search
            norm_now = norm_next
    data_hot = (data_ids[:, None] == vocab_ids).astype(jnp.float32)
    return row_total(jnp.sum((prob - data_hot) * tangent(full_rows(solution)), axis=1))


def solution(mesh):
    placed = (
        P(("groups", "dp"), "fsdp"),
        P(("groups", "dp"), None),
        P(None, "fsdp"),
        P("fsdp"),
        P(None, "fsdp"),
        P(("groups", "dp")),
        P(("groups", "dp")),
    )
    return jax.shard_map(
        per_device, mesh=mesh, in_specs=placed, out_specs=P(("groups", "dp")), check_vma=False
    )
```

profile of v0, /device:TPU:0, one launch (start us, length us, event | category | flops | bytes accessed | tf_op | source)
XLA Modules:
  0.0 1366.7 jit_solution(14872717110527854634)
XLA Ops:
  13.2 23.2 %psum.140 = f32[128,1]{0,1:T(1,128)S(1)} all-reduce(f32[128,1]{0,1:T(1,128)S(1)} %bitcast.129), channel_id=1, replica_groups=mesh['groups'=2,'fsdp'=8,'dp'=2] {'fsdp'}, use_global_device_ids=true, to_apply=%region_1.0 | all-reduce | flops 128 | bytes 1024 | tf_op jit(solution)/shard_map/psum | solution.py:13
  37.2 39.9 %all-gather.10.cloned.1.call-done = bf16[128,5120]{1,0:T(8,128)(2,1)} async-done(((bf16[128,640]{1,0:T(8,128)(2,1)}), bf16[128,5120]{1,0:T(8,128)(2,1)}) %all-gather.10.cloned.1.call-update) | async-done | bytes 1310736 | tf_op jit(solution)/shard_map/all_gather | solution.py:29
  88.4 19.0 %psum.141 = f32[128]{0:T(128)S(1)} all-reduce(f32[128]{0:T(128)S(1)} %get-tuple-element.17), channel_id=1, replica_groups=mesh['groups'=2,'fsdp'=8,'dp'=2] {'fsdp'}, use_global_device_ids=true, to_apply=%region_3.0 | all-reduce | flops 128 | bytes 1024 | tf_op jit(solution)/shard_map/psum | solution.py:13
  120.5 62.6 %reduce-scatter.25.cloned.1.call-done = bf16[640,128]{1,0:T(8,128)(2,1)} async-done(((bf16[5120,128]{1,0:T(8,128)(2,1)}), bf16[640,128]{1,0:T(8,128)(2,1)}) %reduce-scatter.25.cloned.1.call-update) | async-done | bytes 163856
  184.2 19.0 %psum.142 = f32[128,1]{0,1:T(1,128)S(1)} all-reduce(f32[128,1]{0,1:T(1,128)S(1)} %bitcast.130), channel_id=1, replica_groups=mesh['groups'=2,'fsdp'=8,'dp'=2] {'fsdp'}, use_global_device_ids=true, to_apply=%region_6.0 | all-reduce | flops 128 | bytes 1024 | tf_op jit(solution)/shard_map/psum | solution.py:13
  243.5 22.2 %all-gather.12.cloned.1.call-done = bf16[6912,640]{0,1:T(8,128)(2,1)} async-done(((bf16[3456,640]{0,1:T(8,128)(2,1)}), bf16[6912,640]{0,1:T(8,128)(2,1)}) %all-gather.12.cloned.1.call-update) | async-done | bytes 8847376 | tf_op jit(solution)/shard_map/all_gather | solution.py:68
  272.1 21.6 %psum.144 = f32[128,1]{0,1:T(1,128)S(1)} all-reduce(f32[128,1]{0,1:T(1,128)S(1)} %bitcast.134), channel_id=1, replica_groups=mesh['groups'=2,'fsdp'=8,'dp'=2] {'fsdp'}, use_global_device_ids=true, to_apply=%region_11.0 | all-reduce | flops 128 | bytes 1024 | tf_op jit(solution)/shard_map/psum | solution.py:13
  294.6 39.9 %all-gather.14.cloned.1.call-done = bf16[128,5120]{1,0:T(8,128)(2,1)} async-done(((bf16[128,640]{1,0:T(8,128)(2,1)}), bf16[128,5120]{1,0:T(8,128)(2,1)}) %all-gather.14.cloned.1.call-update) | async-done | bytes 1310736 | tf_op jit(solution)/shard_map/all_gather | solution.py:29
  346.0 19.0 %psum.145 = f32[128]{0:T(128)S(1)} all-reduce(f32[128]{0:T(128)S(1)} %get-tuple-element.21), channel_id=1, replica_groups=mesh['groups'=2,'fsdp'=8,'dp'=2] {'fsdp'}, use_global_device_ids=true, to_apply=%region_13.0 | all-reduce | flops 128 | bytes 1024 | tf_op jit(solution)/shard_map/psum | solution.py:13
  378.4 62.5 %reduce-scatter.29.cloned.1.call-done = bf16[640,128]{1,0:T(8,128)(2,1)} async-done(((bf16[5120,128]{1,0:T(8,128)(2,1)}), bf16[640,128]{1,0:T(8,128)(2,1)}) %reduce-scatter.29.cloned.1.call-update) | async-done | bytes 163856
  442.1 19.2 %psum.146 = f32[128,1]{0,1:T(1,128)S(1)} all-reduce(f32[128,1]{0,1:T(1,128)S(1)} %bitcast.131), channel_id=1, replica_groups=mesh['groups'=2,'fsdp'=8,'dp'=2] {'fsdp'}, use_global_device_ids=true, to_apply=%region_16.0 | all-reduce | flops 128 | bytes 1024 | tf_op jit(solution)/shard_map/psum | solution.py:13
  506.5 34.5 %all-reduce = (f32[]{:T(128)}, f32[]{:T(128)}) all-reduce(f32[]{:T(128)} %get-tuple-element.6, f32[]{:T(128)} %get-tuple-element.5), channel_id=1, replica_groups=mesh['groups'=2,'fsdp'=8,'dp'=2] {'fsdp','dp'}, use_global_device_ids=true, to_apply=%region_9.0 | all-reduce | flops 2 | bytes 16 | tf_op jit(solution)/shard_map/psum | solution.py:82
  548.7 30.1 %psum.148 = f32[]{:T(128)} all-reduce(f32[]{:T(128)} %multiply_reduce_fusion.3), channel_id=1, replica_groups=mesh['groups'=2,'fsdp'=8,'dp'=2] {'fsdp','dp'}, use_global_device_ids=true, to_apply=%region_21.0 | all-reduce | flops 1 | bytes 8 | tf_op jit(solution)/shard_map/psum | solution.py:82
  588.4 18.3 %all-gather.16.cloned.1.call-done = bf16[6912,640]{0,1:T(8,128)(2,1)} async-done(((bf16[3456,640]{0,1:T(8,128)(2,1)}), bf16[6912,640]{0,1:T(8,128)(2,1)}) %all-gather.16.cloned.1.call-update) | async-done | bytes 8847376 | tf_op jit(solution)/shard_map/all_gather | solution.py:68
  613.1 21.6 %psum.149 = f32[128,1]{0,1:T(1,128)S(1)} all-reduce(f32[128,1]{0,1:T(1,128)S(1)} %bitcast.135), channel_id=1, replica_groups=mesh['groups'=2,'fsdp'=8,'dp'=2] {'fsdp'}, use_global_device_ids=true, to_apply=%region_23.0 | all-reduce | flops 128 | bytes 1024 | tf_op jit(solution)/shard_map/psum | solution.py:13
  635.6 39.9 %all-gather.18.cloned.1.call-done = bf16[128,5120]{1,0:T(8,128)(2,1)} async-done(((bf16[128,640]{1,0:T(8,128)(2,1)}), bf16[128,5120]{1,0:T(8,128)(2,1)}) %all-gather.18.cloned.1.call-update) | async-done | bytes 1310736 | tf_op jit(solution)/shard_map/all_gather | solution.py:29
  687.0 19.1 %psum.150 = f32[128]{0:T(128)S(1)} all-reduce(f32[128]{0:T(128)S(1)} %get-tuple-element.25), channel_id=1, replica_groups=mesh['groups'=2,'fsdp'=8,'dp'=2] {'fsdp'}, use_global_device_ids=true, to_apply=%region_25.0 | all-reduce | flops 128 | bytes 1024 | tf_op jit(solution)/shard_map/psum | solution.py:13
  719.5 62.5 %reduce-scatter.33.cloned.1.call-done = bf16[640,128]{1,0:T(8,128)(2,1)} async-done(((bf16[5120,128]{1,0:T(8,128)(2,1)}), bf16[640,128]{1,0:T(8,128)(2,1)}) %reduce-scatter.33.cloned.1.call-update) | async-done | bytes 163856
  783.3 19.1 %psum.151 = f32[128,1]{0,1:T(1,128)S(1)} all-reduce(f32[128,1]{0,1:T(1,128)S(1)} %bitcast.132), channel_id=1, replica_groups=mesh['groups'=2,'fsdp'=8,'dp'=2] {'fsdp'}, use_global_device_ids=true, to_apply=%region_28.0 | all-reduce | flops 128 | bytes 1024 | tf_op jit(solution)/shard_map/psum | solution.py:13
  849.7 34.5 %psum.152 = f32[]{:T(128)} all-reduce(f32[]{:T(128)} %multiply_reduce_fusion.2), channel_id=1, replica_groups=mesh['groups'=2,'fsdp'=8,'dp'=2] {'fsdp','dp'}, use_global_device_ids=true, to_apply=%region_31.0 | all-reduce | flops 1 | bytes 8 | tf_op jit(solution)/shard_map/psum | solution.py:82
  893.3 30.3 %psum.153 = f32[]{:T(128)} all-reduce(f32[]{:T(128)} %multiply_reduce_fusion.1), channel_id=1, replica_groups=mesh['groups'=2,'fsdp'=8,'dp'=2] {'fsdp','dp'}, use_global_device_ids=true, to_apply=%region_33.0 | all-reduce | flops 1 | bytes 8 | tf_op jit(solution)/shard_map/psum | solution.py:82
  935.1 18.4 %all-gather.20.cloned.1.call-done = bf16[6912,640]{0,1:T(8,128)(2,1)} async-done(((bf16[3456,640]{0,1:T(8,128)(2,1)}), bf16[6912,640]{0,1:T(8,128)(2,1)}) %all-gather.20.cloned.1.call-update) | async-done | bytes 8847376 | tf_op jit(solution)/shard_map/all_gather | solution.py:68
  959.9 21.6 %psum.154 = f32[128,1]{0,1:T(1,128)S(1)} all-reduce(f32[128,1]{0,1:T(1,128)S(1)} %bitcast.136), channel_id=1, replica_groups=mesh['groups'=2,'fsdp'=8,'dp'=2] {'fsdp'}, use_global_device_ids=true, to_apply=%region_35.0 | all-reduce | flops 128 | bytes 1024 | tf_op jit(solution)/shard_map/psum | solution.py:13
  982.4 39.9 %all-gather.22.cloned.1.call-done = bf16[128,5120]{1,0:T(8,128)(2,1)} async-done(((bf16[128,640]{1,0:T(8,128)(2,1)}), bf16[128,5120]{1,0:T(8,128)(2,1)}) %all-gather.22.cloned.1.call-update) | async-done | bytes 1310736 | tf_op jit(solution)/shard_map/all_gather | solution.py:29
  1033.8 19.0 %psum.155 = f32[128]{0:T(128)S(1)} all-reduce(f32[128]{0:T(128)S(1)} %get-tuple-element.29), channel_id=1, replica_groups=mesh['groups'=2,'fsdp'=8,'dp'=2] {'fsdp'}, use_global_device_ids=true, to_apply=%region_37.0 | all-reduce | flops 128 | bytes 1024 | tf_op jit(solution)/shard_map/psum | solution.py:13
  1066.1 62.5 %reduce-scatter.37.cloned.1.call-done = bf16[640,128]{1,0:T(8,128)(2,1)} async-done(((bf16[5120,128]{1,0:T(8,128)(2,1)}), bf16[640,128]{1,0:T(8,128)(2,1)}) %reduce-scatter.37.cloned.1.call-update) | async-done | bytes 163856
  1129.7 19.5 %psum.156 = f32[128,1]{0,1:T(1,128)S(1)} all-reduce(f32[128,1]{0,1:T(1,128)S(1)} %bitcast.133), channel_id=1, replica_groups=mesh['groups'=2,'fsdp'=8,'dp'=2] {'fsdp'}, use_global_device_ids=true, to_apply=%region_40.0 | all-reduce | flops 128 | bytes 1024 | tf_op jit(solution)/shard_map/psum | solution.py:13
  1196.7 34.5 %psum.157 = f32[]{:T(128)} all-reduce(f32[]{:T(128)} %multiply_reduce_fusion), channel_id=1, replica_groups=mesh['groups'=2,'fsdp'=8,'dp'=2] {'fsdp','dp'}, use_global_device_ids=true, to_apply=%region_43.0 | all-reduce | flops 1 | bytes 8 | tf_op jit(solution)/shard_map/psum | solution.py:82
  1242.1 18.3 %all-gather.24.cloned.1.call-done = bf16[6912,640]{0,1:T(8,128)(2,1)} async-done(((bf16[3456,640]{0,1:T(8,128)(2,1)}), bf16[6912,640]{0,1:T(8,128)(2,1)}) %all-gather.24.cloned.1.call-update) | async-done | bytes 8847376 | tf_op jit(solution)/shard_map/all_gather | solution.py:68
  1266.8 21.9 %psum.158 = f32[128,1]{0,1:T(1,128)S(1)} all-reduce(f32[128,1]{0,1:T(1,128)S(1)} %bitcast.137), channel_id=1, replica_groups=mesh['groups'=2,'fsdp'=8,'dp'=2] {'fsdp'}, use_global_device_ids=true, to_apply=%region_45.0 | all-reduce | flops 128 | bytes 1024 | tf_op jit(solution)/shard_map/psum | solution.py:13
  1289.5 39.9 %all-gather.26.cloned.1.call-done = bf16[128,5120]{1,0:T(8,128)(2,1)} async-done(((bf16[128,640]{1,0:T(8,128)(2,1)}), bf16[128,5120]{1,0:T(8,128)(2,1)}) %all-gather.26.cloned.1.call-update) | async-done | bytes 1310736 | tf_op jit(solution)/shard_map/all_gather | solution.py:29
  1340.2 19.5 %psum.159 = f32[128]{0:T(128)} all-reduce(f32[128]{0:T(128)S(1)} %fusion.21), channel_id=1, replica_groups=mesh['groups'=2,'fsdp'=8,'dp'=2] {'fsdp'}, use_global_device_ids=true, to_apply=%region_47.0 | all-reduce | flops 128 | bytes 1024 | tf_op jit(solution)/shard_map/psum | solution.py:13
  (118 shorter events, 373.7 us)
Async XLA Ops:
  6.5 1.5 copy-start
  6.5 70.6 %all-gather.10.cloned.1.call-start = ((), (), s32[]{:S(2)}) async-start(), calls=%async_computation.8 | async-start | bytes 1474560 | tf_op jit(solution)/shard_map/all_gather | solution.py:29
  37.1 145.9 %reduce-scatter.25.cloned.1.call-start = ((), (), s32[]{:S(2)}) async-start(), calls=%async_computation.17 | async-start | bytes 1474560
  37.2 70.2 %copy-start.5 = (s32[2048]{0:T(1024)}, s32[2048]{0:T(1024)S(1)}, u32[]{:S(2)}) copy-start(s32[2048]{0:T(1024)S(1)} %iota_add_fusion) | copy-start | bytes 24580
  37.2 70.2 %copy-start.7 = (s32[128]{0:T(128)S(1)}, s32[128]{0:T(128)}, u32[]{:S(2)}) copy-start(s32[128]{0:T(128)} %param.13) | copy-start | bytes 1540
  120.4 115.6 %reduce-scatter.27.cloned.1.call-start = ((), (), s32[]{:S(2)}) async-start(), calls=%async_computation.18 | async-start | bytes 13271040
  221.9 43.8 %all-gather.12.cloned.1.call-start = ((), (), s32[]{:S(2)}) async-start(), calls=%async_computation.9 | async-start | bytes 13271040 | tf_op jit(solution)/shard_map/all_gather | solution.py:68
  243.2 91.2 %copy-start.1 = (f32[128,2048]{1,0:T(8,128)S(1)}, f32[128,2048]{1,0:T(8,128)}, u32[]{:S(2)}) copy-start(f32[128,2048]{1,0:T(8,128)} %get-tuple-element.18) | copy-start | bytes 3145732
  243.3 91.2 %all-gather.14.cloned.1.call-start = ((), (), s32[]{:S(2)}) async-start(), calls=%async_computation.10 | async-start | bytes 1474560 | tf_op jit(solution)/shard_map/all_gather | solution.py:29
  294.5 146.3 %reduce-scatter.29.cloned.1.call-start = ((), (), s32[]{:S(2)}) async-start(), calls=%async_computation.19 | async-start | bytes 1474560
  378.4 115.5 %reduce-scatter.31.cloned.1.call-start = ((), (), s32[]{:S(2)}) async-start(), calls=%async_computation.20 | async-start | bytes 13271040
  479.9 126.8 %all-gather.16.cloned.1.call-start = ((), (), s32[]{:S(2)}) async-start(), calls=%async_computation.11 | async-start | bytes 13271040 | tf_op jit(solution)/shard_map/all_gather | solution.py:68
  588.3 87.2 %copy-start.2 = (f32[128,2048]{1,0:T(8,128)S(1)}, f32[128,2048]{1,0:T(8,128)}, u32[]{:S(2)}) copy-start(f32[128,2048]{1,0:T(8,128)} %get-tuple-element.18) | copy-start | bytes 3145732
  588.3 87.2 %all-gather.18.cloned.1.call-start = ((), (), s32[]{:S(2)}) async-start(), calls=%async_computation.12 | async-start | bytes 1474560 | tf_op jit(solution)/shard_map/all_gather | solution.py:29
  635.5 146.6 %reduce-scatter.33.cloned.1.call-start = ((), (), s32[]{:S(2)}) async-start(), calls=%async_computation.21 | async-start | bytes 1474560
  719.5 115.6 %reduce-scatter.35.cloned.1.call-start = ((), (), s32[]{:S(2)}) async-start(), calls=%async_computation.22 | async-start | bytes 13271040
  821.0 132.5 %all-gather.20.cloned.1.call-start = ((), (), s32[]{:S(2)}) async-start(), calls=%async_computation.13 | async-start | bytes 13271040 | tf_op jit(solution)/shard_map/all_gather | solution.py:68
  935.1 87.2 %copy-start.3 = (f32[128,2048]{1,0:T(8,128)S(1)}, f32[128,2048]{1,0:T(8,128)}, u32[]{:S(2)}) copy-start(f32[128,2048]{1,0:T(8,128)} %get-tuple-element.18) | copy-start | bytes 3145732
  935.1 87.2 %all-gather.22.cloned.1.call-start = ((), (), s32[]{:S(2)}) async-start(), calls=%async_computation.14 | async-start | bytes 1474560 | tf_op jit(solution)/shard_map/all_gather | solution.py:29
  982.3 146.2 %reduce-scatter.37.cloned.1.call-start = ((), (), s32[]{:S(2)}) async-start(), calls=%async_computation.23 | async-start | bytes 1474560
  1066.0 115.9 %reduce-scatter.39.cloned.1.call-start = ((), (), s32[]{:S(2)}) async-start(), calls=%async_computation.24 | async-start | bytes 13271040
  1167.8 92.6 %all-gather.24.cloned.1.call-start = ((), (), s32[]{:S(2)}) async-start(), calls=%async_computation.15 | async-start | bytes 13271040 | tf_op jit(solution)/shard_map/all_gather | solution.py:68
  1242.0 87.5 %copy-start.4 = (f32[128,2048]{1,0:T(8,128)S(1)}, f32[128,2048]{1,0:T(8,128)}, u32[]{:S(2)}) copy-start(f32[128,2048]{1,0:T(8,128)} %get-tuple-element.18) | copy-start | bytes 3145732
  1242.0 87.5 %copy-start.6 = (s32[2048]{0:T(1024)S(1)}, s32[2048]{0:T(1024)}, u32[]{:S(2)}) copy-start(s32[2048]{0:T(1024)} %copy-done.5) | copy-start | bytes 24580
  1242.0 87.5 %copy-start.8 = (s32[128]{0:T(128)S(1)}, s32[128]{0:T(128)}, u32[]{:S(2)}) copy-start(s32[128]{0:T(128)} %param.12) | copy-start | bytes 1540
  1242.0 87.4 %all-gather.26.cloned.1.call-start = ((), (), s32[]{:S(2)}) async-start(), calls=%async_computation.16 | async-start | bytes 1474560 | tf_op jit(solution)/shard_map/all_gather | solution.py:29
Sparse Core Ops, SparseCore 0:
  37.2 39.7 all-gather.9
  120.5 62.4 reduce-scatter.24
  222.0 13.9 reduce-scatter.26
  243.4 22.2 all-gather.11
  294.6 39.7 all-gather.13
  378.5 62.3 reduce-scatter.28
  480.0 13.8 reduce-scatter.30
  588.4 18.2 all-gather.15
  635.6 39.7 all-gather.17
  719.6 62.4 reduce-scatter.32
  821.1 13.9 reduce-scatter.34
  935.2 18.2 all-gather.19
  982.4 39.7 all-gather.21
  1066.1 62.3 reduce-scatter.36
  1167.9 13.9 reduce-scatter.38
  1242.1 18.2 all-gather.23
  1289.6 39.7 all-gather.25
where the time goes:
time: 1380 us; the launch traced here: 1370 us
  waiting for transfers between devices  583 us (42%)
  blocking collectives  446 us (32%)
  matrix products  159 us (12%)
  local copies, waits for them, and re-layouts  89.8 us (7%)
  other arithmetic  68 us (5%)
  between operations  20.3 us (1%)
    unnamed x25, waiting for transfers between devices  306 us
    psum x14, blocking collectives, row_total(): return lax.psum(values, 'fsdp')  282 us
    all_gather x5, waiting for transfers between devices, head_logits(): lax.all_gather(normed_shard, 'fsdp', axis=1, tiled=True)  199 us
    psum x5, blocking collectives, global_dot(): return lax.psum(values, ('fsdp', 'dp'))  164 us
    unnamed x34, local copies, waits for them, and re-layouts  89.8 us
    all_gather x4, waiting for transfers between devices, full_rows(): return lax.all_gather(vector.astype(jnp.bfloat16), 'dp', axis=0, tiled=True)  77.2 us
    dot_general x5, matrix products, head_logits(): jnp.dot(lax.all_gather(normed_shard, 'fsdp', axis=1, tiled=True), head, p...  56.8 us
    dot_general x4, matrix products, head_project(): lax.dot_general(head, weighted, (((1,), (1,)), ((), ())), preferred_eleme...  47 us
  transfers between devices with their start and end apart: 17, of which 17 were waited for; matrix products, arithmetic and copies ran while one was open for 0% of the time, Pallas kernels for 0%

commit v1 on v0

--- a/solution.py
+++ b/solution.py
@@ -79,7 +79,7 @@
         ).astype(jnp.float32)
 
     def global_dot(values):
-        return lax.psum(values, ("fsdp", "dp"))
+        return lax.psum(lax.psum(values, "dp"), "fsdp")
 
     pseudo_hot = (pseudo_ids[:, None] == vocab_ids).astype(jnp.float32)
     grad = param_sum(norm_back((prob - pseudo_hot) / total_rows))

time: 1380 us -> 1330 us (0.964)
  blocking collectives: 446 us -> 400 us
    psum x5 -> x10, blocking collectives: 164 us -> 118 us  [global_dot(): return lax.psum(lax.psum(values, 'dp'), 'fsdp')]
where the time goes in v1:
time: 1330 us; the launch traced here: 1320 us
  waiting for transfers between devices  585 us (44%)
  blocking collectives  400 us (30%)
  matrix products  159 us (12%)
  local copies, waits for them, and re-layouts  89.8 us (7%)
  other arithmetic  67.9 us (5%)
  between operations  20 us (2%)
    unnamed x25, waiting for transfers between devices  306 us
    psum x14, blocking collectives, row_total(): return lax.psum(values, 'fsdp')  282 us
    all_gather x5, waiting for transfers between devices, head_logits(): lax.all_gather(normed_shard, 'fsdp', axis=1, tiled=True)  199 us
    psum x10, blocking collectives, global_dot(): return lax.psum(lax.psum(values, 'dp'), 'fsdp')  118 us
    unnamed x34, local copies, waits for them, and re-layouts  89.8 us
    all_gather x4, waiting for transfers between devices, full_rows(): return lax.all_gather(vector.astype(jnp.bfloat16), 'dp', axis=0, tiled=True)  79.8 us
    dot_general x5, matrix products, head_logits(): jnp.dot(lax.all_gather(normed_shard, 'fsdp', axis=1, tiled=True), head, p...  56.8 us
    dot_general x4, matrix products, head_project(): lax.dot_general(head, weighted, (((1,), (1,)), ((), ())), preferred_eleme...  47 us
  transfers between devices with their start and end apart: 17, of which 17 were waited for; matrix products, arithmetic and copies ran while one was open for 0% of the time, Pallas kernels for 0%

profile of v1, /device:TPU:0, one launch (start us, length us, event | category | flops | bytes accessed | tf_op | source)
XLA Modules:
  0.0 1323.1 jit_solution(2709484673725657721)
XLA Ops:
  13.2 23.2 %psum.182 = f32[128,1]{0,1:T(1,128)S(1)} all-reduce(f32[128,1]{0,1:T(1,128)S(1)} %bitcast.129), channel_id=1, replica_groups=mesh['groups'=2,'fsdp'=8,'dp'=2] {'fsdp'}, use_global_device_ids=true, to_apply=%region_1.0 | all-reduce | flops 128 | bytes 1024 | tf_op jit(solution)/shard_map/psum | solution.py:13
  37.2 39.9 %all-gather.10.cloned.1.call-done = bf16[128,5120]{1,0:T(8,128)(2,1)} async-done(((bf16[128,640]{1,0:T(8,128)(2,1)}), bf16[128,5120]{1,0:T(8,128)(2,1)}) %all-gather.10.cloned.1.call-update) | async-done | bytes 1310736 | tf_op jit(solution)/shard_map/all_gather | solution.py:29
  88.4 19.0 %psum.183 = f32[128]{0:T(128)S(1)} all-reduce(f32[128]{0:T(128)S(1)} %get-tuple-element.19), channel_id=1, replica_groups=mesh['groups'=2,'fsdp'=8,'dp'=2] {'fsdp'}, use_global_device_ids=true, to_apply=%region_3.0 | all-reduce | flops 128 | bytes 1024 | tf_op jit(solution)/shard_map/psum | solution.py:13
  120.4 62.4 %reduce-scatter.25.cloned.1.call-done = bf16[640,128]{1,0:T(8,128)(2,1)} async-done(((bf16[5120,128]{1,0:T(8,128)(2,1)}), bf16[640,128]{1,0:T(8,128)(2,1)}) %reduce-scatter.25.cloned.1.call-update) | async-done | bytes 163856
  184.1 19.1 %psum.184 = f32[128,1]{0,1:T(1,128)S(1)} all-reduce(f32[128,1]{0,1:T(1,128)S(1)} %bitcast.130), channel_id=1, replica_groups=mesh['groups'=2,'fsdp'=8,'dp'=2] {'fsdp'}, use_global_device_ids=true, to_apply=%region_6.0 | all-reduce | flops 128 | bytes 1024 | tf_op jit(solution)/shard_map/psum | solution.py:13
  243.5 22.1 %all-gather.12.cloned.1.call-done = bf16[6912,640]{0,1:T(8,128)(2,1)} async-done(((bf16[3456,640]{0,1:T(8,128)(2,1)}), bf16[6912,640]{0,1:T(8,128)(2,1)}) %all-gather.12.cloned.1.call-update) | async-done | bytes 8847376 | tf_op jit(solution)/shard_map/all_gather | solution.py:68
  271.9 21.6 %psum.187 = f32[128,1]{0,1:T(1,128)S(1)} all-reduce(f32[128,1]{0,1:T(1,128)S(1)} %bitcast.134), channel_id=1, replica_groups=mesh['groups'=2,'fsdp'=8,'dp'=2] {'fsdp'}, use_global_device_ids=true, to_apply=%region_12.0 | all-reduce | flops 128 | bytes 1024 | tf_op jit(solution)/shard_map/psum | solution.py:13
  294.5 39.9 %all-gather.14.cloned.1.call-done = bf16[128,5120]{1,0:T(8,128)(2,1)} async-done(((bf16[128,640]{1,0:T(8,128)(2,1)}), bf16[128,5120]{1,0:T(8,128)(2,1)}) %all-gather.14.cloned.1.call-update) | async-done | bytes 1310736 | tf_op jit(solution)/shard_map/all_gather | solution.py:29
  345.9 19.0 %psum.188 = f32[128]{0:T(128)S(1)} all-reduce(f32[128]{0:T(128)S(1)} %get-tuple-element.23), channel_id=1, replica_groups=mesh['groups'=2,'fsdp'=8,'dp'=2] {'fsdp'}, use_global_device_ids=true, to_apply=%region_14.0 | all-reduce | flops 128 | bytes 1024 | tf_op jit(solution)/shard_map/psum | solution.py:13
  378.3 62.5 %reduce-scatter.29.cloned.1.call-done = bf16[640,128]{1,0:T(8,128)(2,1)} async-done(((bf16[5120,128]{1,0:T(8,128)(2,1)}), bf16[640,128]{1,0:T(8,128)(2,1)}) %reduce-scatter.29.cloned.1.call-update) | async-done | bytes 163856
  441.9 19.2 %psum.189 = f32[128,1]{0,1:T(1,128)S(1)} all-reduce(f32[128,1]{0,1:T(1,128)S(1)} %bitcast.131), channel_id=1, replica_groups=mesh['groups'=2,'fsdp'=8,'dp'=2] {'fsdp'}, use_global_device_ids=true, to_apply=%region_17.0 | all-reduce | flops 128 | bytes 1024 | tf_op jit(solution)/shard_map/psum | solution.py:13
  509.5 22.4 %all-reduce = (f32[]{:T(128)}, f32[]{:T(128)}) all-reduce(f32[]{:T(128)} %get-tuple-element.9, f32[]{:T(128)} %get-tuple-element.10), channel_id=1, replica_groups=mesh['groups'=2,'fsdp'=8,'dp'=2] {'fsdp'}, use_global_device_ids=true, to_apply=%region_10.0 | all-reduce | flops 2 | bytes 16 | tf_op jit(solution)/shard_map/psum | solution.py:82
  542.6 17.7 %psum.193 = f32[]{:T(128)} all-reduce(f32[]{:T(128)} %psum.192), channel_id=1, replica_groups=mesh['groups'=2,'fsdp'=8,'dp'=2] {'fsdp'}, use_global_device_ids=true, to_apply=%region_24.0 | all-reduce | flops 1 | bytes 8 | tf_op jit(solution)/shard_map/psum | solution.py:82
  569.9 19.8 %all-gather.16.cloned.1.call-done = bf16[6912,640]{0,1:T(8,128)(2,1)} async-done(((bf16[3456,640]{0,1:T(8,128)(2,1)}), bf16[6912,640]{0,1:T(8,128)(2,1)}) %all-gather.16.cloned.1.call-update) | async-done | bytes 8847376 | tf_op jit(solution)/shard_map/all_gather | solution.py:68
  596.1 21.6 %psum.194 = f32[128,1]{0,1:T(1,128)S(1)} all-reduce(f32[128,1]{0,1:T(1,128)S(1)} %bitcast.135), channel_id=1, replica_groups=mesh['groups'=2,'fsdp'=8,'dp'=2] {'fsdp'}, use_global_device_ids=true, to_apply=%region_26.0 | all-reduce | flops 128 | bytes 1024 | tf_op jit(solution)/shard_map/psum | solution.py:13
  618.8 39.7 %all-gather.18.cloned.1.call-done = bf16[128,5120]{1,0:T(8,128)(2,1)} async-done(((bf16[128,640]{1,0:T(8,128)(2,1)}), bf16[128,5120]{1,0:T(8,128)(2,1)}) %all-gather.18.cloned.1.call-update) | async-done | bytes 1310736 | tf_op jit(solution)/shard_map/all_gather | solution.py:29
  670.0 19.0 %psum.195 = f32[128]{0:T(128)S(1)} all-reduce(f32[128]{0:T(128)S(1)} %get-tuple-element.27), channel_id=1, replica_groups=mesh['groups'=2,'fsdp'=8,'dp'=2] {'fsdp'}, use_global_device_ids=true, to_apply=%region_28.0 | all-reduce | flops 128 | bytes 1024 | tf_op jit(solution)/shard_map/psum | solution.py:13
  702.4 62.5 %reduce-scatter.33.cloned.1.call-done = bf16[640,128]{1,0:T(8,128)(2,1)} async-done(((bf16[5120,128]{1,0:T(8,128)(2,1)}), bf16[640,128]{1,0:T(8,128)(2,1)}) %reduce-scatter.33.cloned.1.call-update) | async-done | bytes 163856
  766.0 19.1 %psum.196 = f32[128,1]{0,1:T(1,128)S(1)} all-reduce(f32[128,1]{0,1:T(1,128)S(1)} %bitcast.132), channel_id=1, replica_groups=mesh['groups'=2,'fsdp'=8,'dp'=2] {'fsdp'}, use_global_device_ids=true, to_apply=%region_31.0 | all-reduce | flops 128 | bytes 1024 | tf_op jit(solution)/shard_map/psum | solution.py:13
  835.6 22.6 %psum.198 = f32[]{:T(128)} all-reduce(f32[]{:T(128)} %psum.197), channel_id=1, replica_groups=mesh['groups'=2,'fsdp'=8,'dp'=2] {'fsdp'}, use_global_device_ids=true, to_apply=%region_35.0 | all-reduce | flops 1 | bytes 8 | tf_op jit(solution)/shard_map/psum | solution.py:82
  870.4 17.8 %psum.200 = f32[]{:T(128)} all-reduce(f32[]{:T(128)} %psum.199), channel_id=1, replica_groups=mesh['groups'=2,'fsdp'=8,'dp'=2] {'fsdp'}, use_global_device_ids=true, to_apply=%region_38.0 | all-reduce | flops 1 | bytes 8 | tf_op jit(solution)/shard_map/psum | solution.py:82
  899.7 19.8 %all-gather.20.cloned.1.call-done = bf16[6912,640]{0,1:T(8,128)(2,1)} async-done(((bf16[3456,640]{0,1:T(8,128)(2,1)}), bf16[6912,640]{0,1:T(8,128)(2,1)}) %all-gather.20.cloned.1.call-update) | async-done | bytes 8847376 | tf_op jit(solution)/shard_map/all_gather | solution.py:68
  925.8 21.6 %psum.201 = f32[128,1]{0,1:T(1,128)S(1)} all-reduce(f32[128,1]{0,1:T(1,128)S(1)} %bitcast.136), channel_id=1, replica_groups=mesh['groups'=2,'fsdp'=8,'dp'=2] {'fsdp'}, use_global_device_ids=true, to_apply=%region_40.0 | all-reduce | flops 128 | bytes 1024 | tf_op jit(solution)/shard_map/psum | solution.py:13
  948.3 39.9 %all-gather.22.cloned.1.call-done = bf16[128,5120]{1,0:T(8,128)(2,1)} async-done(((bf16[128,640]{1,0:T(8,128)(2,1)}), bf16[128,5120]{1,0:T(8,128)(2,1)}) %all-gather.22.cloned.1.call-update) | async-done | bytes 1310736 | tf_op jit(solution)/shard_map/all_gather | solution.py:29
  999.7 19.4 %psum.202 = f32[128]{0:T(128)S(1)} all-reduce(f32[128]{0:T(128)S(1)} %get-tuple-element.31), channel_id=1, replica_groups=mesh['groups'=2,'fsdp'=8,'dp'=2] {'fsdp'}, use_global_device_ids=true, to_apply=%region_42.0 | all-reduce | flops 128 | bytes 1024 | tf_op jit(solution)/shard_map/psum | solution.py:13
  1032.4 62.4 %reduce-scatter.37.cloned.1.call-done = bf16[640,128]{1,0:T(8,128)(2,1)} async-done(((bf16[5120,128]{1,0:T(8,128)(2,1)}), bf16[640,128]{1,0:T(8,128)(2,1)}) %reduce-scatter.37.cloned.1.call-update) | async-done | bytes 163856
  1096.0 19.3 %psum.203 = f32[128,1]{0,1:T(1,128)S(1)} all-reduce(f32[128,1]{0,1:T(1,128)S(1)} %bitcast.133), channel_id=1, replica_groups=mesh['groups'=2,'fsdp'=8,'dp'=2] {'fsdp'}, use_global_device_ids=true, to_apply=%region_45.0 | all-reduce | flops 128 | bytes 1024 | tf_op jit(solution)/shard_map/psum | solution.py:13
  1165.8 22.3 %psum.205 = f32[]{:T(128)} all-reduce(f32[]{:T(128)} %psum.204), channel_id=1, replica_groups=mesh['groups'=2,'fsdp'=8,'dp'=2] {'fsdp'}, use_global_device_ids=true, to_apply=%region_49.0 | all-reduce | flops 1 | bytes 8 | tf_op jit(solution)/shard_map/psum | solution.py:82
  1199.2 18.2 %all-gather.24.cloned.1.call-done = bf16[6912,640]{0,1:T(8,128)(2,1)} async-done(((bf16[3456,640]{0,1:T(8,128)(2,1)}), bf16[6912,640]{0,1:T(8,128)(2,1)}) %all-gather.24.cloned.1.call-update) | async-done | bytes 8847376 | tf_op jit(solution)/shard_map/all_gather | solution.py:68
  1223.8 21.6 %psum.206 = f32[128,1]{0,1:T(1,128)S(1)} all-reduce(f32[128,1]{0,1:T(1,128)S(1)} %bitcast.137), channel_id=1, replica_groups=mesh['groups'=2,'fsdp'=8,'dp'=2] {'fsdp'}, use_global_device_ids=true, to_apply=%region_51.0 | all-reduce | flops 128 | bytes 1024 | tf_op jit(solution)/shard_map/psum | solution.py:13
  1246.2 40.0 %all-gather.26.cloned.1.call-done = bf16[128,5120]{1,0:T(8,128)(2,1)} async-done(((bf16[128,640]{1,0:T(8,128)(2,1)}), bf16[128,5120]{1,0:T(8,128)(2,1)}) %all-gather.26.cloned.1.call-update) | async-done | bytes 1310736 | tf_op jit(solution)/shard_map/all_gather | solution.py:29
  1296.9 19.5 %psum.207 = f32[128]{0:T(128)} all-reduce(f32[128]{0:T(128)S(1)} %fusion.21), channel_id=1, replica_groups=mesh['groups'=2,'fsdp'=8,'dp'=2] {'fsdp'}, use_global_device_ids=true, to_apply=%region_53.0 | all-reduce | flops 128 | bytes 1024 | tf_op jit(solution)/shard_map/psum | solution.py:13
  (123 shorter events, 389.4 us)
Async XLA Ops:
  6.5 1.5 copy-start
  6.5 70.6 %all-gather.10.cloned.1.call-start = ((), (), s32[]{:S(2)}) async-start(), calls=%async_computation.8 | async-start | bytes 1474560 | tf_op jit(solution)/shard_map/all_gather | solution.py:29
  37.1 145.8 %reduce-scatter.25.cloned.1.call-start = ((), (), s32[]{:S(2)}) async-start(), calls=%async_computation.17 | async-start | bytes 1474560
  37.2 70.2 %copy-start.5 = (s32[2048]{0:T(1024)}, s32[2048]{0:T(1024)S(1)}, u32[]{:S(2)}) copy-start(s32[2048]{0:T(1024)S(1)} %iota_add_fusion) | copy-start | bytes 24580
  37.2 70.2 %copy-start.7 = (s32[128]{0:T(128)S(1)}, s32[128]{0:T(128)}, u32[]{:S(2)}) copy-start(s32[128]{0:T(128)} %param.13) | copy-start | bytes 1540
  120.4 115.5 %reduce-scatter.27.cloned.1.call-start = ((), (), s32[]{:S(2)}) async-start(), calls=%async_computation.18 | async-start | bytes 13271040
  221.8 43.8 %all-gather.12.cloned.1.call-start = ((), (), s32[]{:S(2)}) async-start(), calls=%async_computation.9 | async-start | bytes 13271040 | tf_op jit(solution)/shard_map/all_gather | solution.py:68
  243.1 91.3 %copy-start.1 = (f32[128,2048]{1,0:T(8,128)S(1)}, f32[128,2048]{1,0:T(8,128)}, u32[]{:S(2)}) copy-start(f32[128,2048]{1,0:T(8,128)} %get-tuple-element.20) | copy-start | bytes 3145732
  243.1 91.2 %all-gather.14.cloned.1.call-start = ((), (), s32[]{:S(2)}) async-start(), calls=%async_computation.10 | async-start | bytes 1474560 | tf_op jit(solution)/shard_map/all_gather | solution.py:29
  294.4 146.3 %reduce-scatter.29.cloned.1.call-start = ((), (), s32[]{:S(2)}) async-start(), calls=%async_computation.19 | async-start | bytes 1474560
  378.2 115.5 %reduce-scatter.31.cloned.1.call-start = ((), (), s32[]{:S(2)}) async-start(), calls=%async_computation.20 | async-start | bytes 13271040
  479.8 109.9 %all-gather.16.cloned.1.call-start = ((), (), s32[]{:S(2)}) async-start(), calls=%async_computation.11 | async-start | bytes 13271040 | tf_op jit(solution)/shard_map/all_gather | solution.py:68
  569.9 88.6 %copy-start.2 = (f32[128,2048]{1,0:T(8,128)S(1)}, f32[128,2048]{1,0:T(8,128)}, u32[]{:S(2)}) copy-start(f32[128,2048]{1,0:T(8,128)} %get-tuple-element.20) | copy-start | bytes 3145732
  569.9 88.6 %all-gather.18.cloned.1.call-start = ((), (), s32[]{:S(2)}) async-start(), calls=%async_computation.12 | async-start | bytes 1474560 | tf_op jit(solution)/shard_map/all_gather | solution.py:29
  618.5 146.3 %reduce-scatter.33.cloned.1.call-start = ((), (), s32[]{:S(2)}) async-start(), calls=%async_computation.21 | async-start | bytes 1474560
  702.3 115.6 %reduce-scatter.35.cloned.1.call-start = ((), (), s32[]{:S(2)}) async-start(), calls=%async_computation.22 | async-start | bytes 13271040
  803.8 115.6 %all-gather.20.cloned.1.call-start = ((), (), s32[]{:S(2)}) async-start(), calls=%async_computation.13 | async-start | bytes 13271040 | tf_op jit(solution)/shard_map/all_gather | solution.py:68
  899.6 88.6 %copy-start.3 = (f32[128,2048]{1,0:T(8,128)S(1)}, f32[128,2048]{1,0:T(8,128)}, u32[]{:S(2)}) copy-start(f32[128,2048]{1,0:T(8,128)} %get-tuple-element.20) | copy-start | bytes 3145732
  899.6 88.6 %all-gather.22.cloned.1.call-start = ((), (), s32[]{:S(2)}) async-start(), calls=%async_computation.14 | async-start | bytes 1474560 | tf_op jit(solution)/shard_map/all_gather | solution.py:29
  948.2 146.6 %reduce-scatter.37.cloned.1.call-start = ((), (), s32[]{:S(2)}) async-start(), calls=%async_computation.23 | async-start | bytes 1474560
  1032.3 115.6 %reduce-scatter.39.cloned.1.call-start = ((), (), s32[]{:S(2)}) async-start(), calls=%async_computation.24 | async-start | bytes 13271040
  1133.9 83.5 %all-gather.24.cloned.1.call-start = ((), (), s32[]{:S(2)}) async-start(), calls=%async_computation.15 | async-start | bytes 13271040 | tf_op jit(solution)/shard_map/all_gather | solution.py:68
  1198.9 87.2 %copy-start.4 = (f32[128,2048]{1,0:T(8,128)S(1)}, f32[128,2048]{1,0:T(8,128)}, u32[]{:S(2)}) copy-start(f32[128,2048]{1,0:T(8,128)} %get-tuple-element.20) | copy-start | bytes 3145732
  1199.0 87.2 %copy-start.6 = (s32[2048]{0:T(1024)S(1)}, s32[2048]{0:T(1024)}, u32[]{:S(2)}) copy-start(s32[2048]{0:T(1024)} %copy-done.5) | copy-start | bytes 24580
  1199.0 87.2 %copy-start.8 = (s32[128]{0:T(128)S(1)}, s32[128]{0:T(128)}, u32[]{:S(2)}) copy-start(s32[128]{0:T(128)} %param.12) | copy-start | bytes 1540
  1199.0 87.2 %all-gather.26.cloned.1.call-start = ((), (), s32[]{:S(2)}) async-start(), calls=%async_computation.16 | async-start | bytes 1474560 | tf_op jit(solution)/shard_map/all_gather | solution.py:29
Sparse Core Ops, SparseCore 0:
  37.2 39.8 all-gather.9
  120.5 62.3 reduce-scatter.24
  221.9 13.9 reduce-scatter.26
  243.2 22.2 all-gather.11
  294.5 39.7 all-gather.13
  378.4 62.3 reduce-scatter.28
  479.9 13.8 reduce-scatter.30
  570.0 19.6 all-gather.15
  618.7 39.7 all-gather.17
  702.5 62.3 reduce-scatter.32
  803.9 13.9 reduce-scatter.34
  899.7 19.6 all-gather.19
  948.4 39.7 all-gather.21
  1032.5 62.2 reduce-scatter.36
  1134.0 13.8 reduce-scatter.38
  1199.1 18.2 all-gather.23
  1246.3 39.7 all-gather.25
